TPU v7x, 128 devices: a whole 4x4x4 slice. The times are simulated.
128 devices in a mesh: rows: 16 (over x, y), cols: 8 (over z, core).
Axes of the slice: x: 4, y: 4, z: 4, core: 2. Of those that a mesh axis runs over, the one named last changes fastest.
Arguments:
- projection: float32 [8192, 65536], P('rows', 'cols'), may hold values from -0.0625 to 0.0625
- basis: float32 [128, 65536], P(None, ('cols', 'rows')), may hold values from -6 to 6
Outputs:
- new_block: float32 [16, 65536], P(None, ('cols', 'rows'))
- coefficients: float32 [128, 16], replicated
- factor: float32 [16, 16], replicated
All inputs are finite; a program needn't handle non-finite values.
Results may differ from a plain program's by a relative error of at most 0.0029.
Values sent between devices are 32-bit elements; how exact they have to be, the bound alone decides.
A program may use at most 64 MiB of HBM per device.

v0:
```python
import jax
import jax.numpy as jnp
from jax import lax
from jax.sharding import PartitionSpec as P

N = 65536
BS = 16


def from_everyone(array, axis):
    copies = jnp.broadcast_to(array, (lax.axis_size(axis), *array.shape))
    return lax.all_to_all(copies, axis, split_axis=0, concat_axis=0, tiled=True)


def taken_together(array, axis):
    everything = from_everyone(array, axis)
    return jnp.sum(everything, axis=0)


def in_order(tiles, dim):
    tiles = jnp.moveaxis(tiles, 0, dim)
    shape = tiles.shape
    return tiles.reshape(*shape[:dim], shape[dim] * shape[dim + 1], *shape[dim + 2 :])


def collect(array, axis, dim):
    tiles = from_everyone(array, axis)
    return in_order(tiles, dim)


def split_up(array, dim, devices):
    shape = array.shape
    tiles = array.reshape(*shape[:dim], devices, shape[dim] // devices, *shape[dim + 1 :])
    return jnp.moveaxis(tiles, dim, 0)


def sum_at_owner(array, axis, dim):
    tiles = split_up(array, dim, lax.axis_size(axis))
    arrived = lax.all_to_all(tiles, axis, split_axis=0, concat_axis=0, tiled=True)
    return arrived.sum(axis=0)


def rows_for(lines, devices):
    spare = -lines.shape[0] % devices
    if not spare:
        return lines
    return jnp.concatenate([lines, jnp.zeros((spare, *lines.shape[1:]), lines.dtype)])


def sum_by_parts(array, axes):
    lines = array.reshape(-1, array.shape[-1])
    own = sum_at_owner(rows_for(lines, lax.axis_size(axes)), axes, 0)
    whole = collect(own, axes, 0)
    return whole[: len(lines)].reshape(array.shape)


def contract(left, right):
    return lax.dot_general(
        left,
        right,
        (((1,), (1,)), ((), ())),
        precision=lax.Precision.HIGHEST,
        preferred_element_type=jnp.float32,
    )


def matmul(left, right):
    return jnp.dot(left, right, precision=lax.Precision.HIGHEST, preferred_element_type=jnp.float32)


def narrow_reduce(values):
    return jax.tree.map(lambda part: taken_together(part, "cols"), values)


def orthogonalize(vectors, image, reducer):
    cross, correlation, self_gram = reducer(
        (contract(vectors, image), contract(vectors, vectors), contract(image, image))
    )
    cross = cross / N
    correlation = correlation / N
    self_gram = self_gram / N
    coeffs = cross + (cross - matmul(correlation, cross))
    gram_matrix = (
        self_gram
        - matmul(cross.T, coeffs)
        - matmul(coeffs.T, cross)
        + matmul(coeffs.T, matmul(correlation, coeffs))
    )
    image_two = image - matmul(coeffs.T, vectors)
    factor = jnp.linalg.cholesky(gram_matrix)
    new_block = jax.scipy.linalg.solve_triangular(factor, image_two, lower=True)
    return (new_block, coeffs, factor)


def local(projection, basis):
    current = basis[basis.shape[0] - BS :]
    partial_value = contract(collect(current, "rows", 1), projection)
    projected = taken_together(partial_value, "cols")
    image = matmul(projected, projection)
    adjoint = sum_by_parts(image, "rows")
    vectors = lax.all_gather(basis, "rows", axis=1, tiled=True)
    new_block, coeffs, factor = orthogonalize(vectors, adjoint, narrow_reduce)
    piece_cols = basis.shape[1]
    own_piece = lax.dynamic_slice_in_dim(
        new_block, lax.axis_index("rows") * piece_cols, piece_cols, 1
    )
    return (own_piece, coeffs, factor)


def solution(mesh):
    placed = (P("rows", "cols"), P(None, ("cols", "rows")))
    return jax.shard_map(
        local,
        mesh=mesh,
        in_specs=placed,
        out_specs=(P(None, ("cols", "rows")), P(), P()),
        check_vma=False,
    )
```

profile of v0, /device:TPU:1, one launch (start us, length us, event | category | flops | bytes accessed | tf_op | source)
XLA Modules:
  0.0 153.9 jit_solution(3380864361591639636)
XLA Ops:
  7.2 0.7 all-gather.2.cloned.1.call-update
  7.9 0.8 slice.15
  8.7 17.7 %all_to_all.35 = f32[16,16,512]{2,1,0:T(8,128)S(1)} all-to-all(f32[16,16,512]{2,1,0:T(8,128)S(1)} %broadcast_in_dim.20), channel_id=1, replica_groups=mesh['rows'=16,'cols'=8] {'rows'}, dimensions={0} | all-to-all | bytes 1048576 | tf_op jit(solution)/shard_map/all_to_all | solution.py:12
  26.4 16.7 %fusion.24 = f32[16,512]{1,0:T(8,128)S(1)} fusion(f32[16,8192]{1,0:T(8,128)S(1)} %bitcast.37, f32[512,8192]{1,0:T(8,128)} %param.2), kind=kOutput, calls=%fused_computation.39 | convolution fusion | flops 805306368 | bytes 17334272 | tf_op jit(solution)/shard_map/dot_general | solution.py:58
  43.2 13.9 %all_to_all.36 = f32[8,16,512]{2,1,0:T(8,128)S(1)} all-to-all(f32[8,16,512]{2,1,0:T(8,128)S(1)} %broadcast_in_dim.21), channel_id=1, replica_groups=mesh['rows'=16,'cols'=8] {'cols'}, dimensions={0} | all-to-all | bytes 524288 | tf_op jit(solution)/shard_map/all_to_all | solution.py:12
  57.1 11.6 %convolution_bitcast_fusion = f32[16,1,8192]{2,0,1:T(8,128)S(1)} fusion(f32[16,512]{1,0:T(8,128)S(1)} %reduce_sum.45, f32[512,8192]{1,0:T(8,128)} %param.2), kind=kOutput, calls=%fused_computation.1 | convolution fusion | flops 805306368 | bytes 17334272 | tf_op jit(solution)/shard_map/dot_general | solution.py:68
  69.2 11.9 %all_to_all.37 = f32[16,1,8192]{2,1,0:T(1,128)S(1)} all-to-all(f32[16,1,8192]{2,1,0:T(1,128)S(1)} %copy.28), channel_id=1, replica_groups=mesh['rows'=16,'cols'=8] {'rows'}, dimensions={0} | all-to-all | bytes 1048576 | tf_op jit(solution)/shard_map/all_to_all | solution.py:39
  81.9 13.5 %all_to_all.38 = f32[16,1,8192]{2,1,0:T(1,128)S(1)} all-to-all(f32[16,1,8192]{2,1,0:T(1,128)S(1)} %broadcast_in_dim.22), channel_id=1, replica_groups=mesh['rows'=16,'cols'=8] {'rows'}, dimensions={0} | all-to-all | bytes 1048576 | tf_op jit(solution)/shard_map/all_to_all | solution.py:12
  95.4 1.0 fusion.2
  96.4 0.7 reshape.31
  97.1 6.6 %all-to-all-start.4 = ((f32[8,1,256]{2,1,0:T(1,128)}), f32[8,1,256]{2,1,0:T(1,128)S(1)}, u32[]{:S(2)}, u32[]{:S(2)}) async-start(f32[8,1,256]{2,1,0:T(1,128)} %reshape.31), calls=%async_computation.4 | async-start | bytes 16384 | tf_op jit(solution)/shard_map/all_to_all | solution.py:12
  103.7 5.1 %convolution_bitcast_fusion.1 = f32[128,16]{0,1:T(8,128)S(1)} fusion(f32[128,8192]{1,0:T(8,128)} %all-gather.2.cloned.1.call-done, f32[16,1,8192]{2,1,0:T(1,128)S(1)} %all_to_all.38), kind=kOutput, calls=%fused_computation.7 | convolution fusion | flops 201326592 | bytes 4726784 | tf_op jit(solution)/shard_map/dot_general | solution.py:58
  108.8 0.6 broadcast_in_dim.24
  109.4 4.8 %all-to-all-start.5 = ((f32[8,128,16]{1,2,0:T(8,128)}), f32[8,128,16]{1,2,0:T(8,128)S(1)}, u32[]{:S(2)}, u32[]{:S(2)}) async-start(f32[8,128,16]{1,2,0:T(8,128)} %broadcast_in_dim.24), calls=%async_computation.5 | async-start | bytes 131072 | tf_op jit(solution)/shard_map/all_to_all | solution.py:12
  114.2 7.0 %fusion.25 = f32[128,128]{1,0:T(8,128)S(1)} fusion(f32[128,8192]{1,0:T(8,128)} %all-gather.2.cloned.1.call-done), kind=kOutput, calls=%fused_computation.40 | convolution fusion | flops 1610612736 | bytes 4259840 | tf_op jit(solution)/shard_map/dot_general | solution.py:58
  121.2 0.8 broadcast_in_dim.25
  122.0 4.8 %all-to-all-start.6 = ((f32[8,128,128]{2,1,0:T(8,128)}), f32[8,128,128]{2,1,0:T(8,128)S(1)}, u32[]{:S(2)}, u32[]{:S(2)}) async-start(f32[8,128,128]{2,1,0:T(8,128)} %broadcast_in_dim.25), calls=%async_computation.6 | async-start | bytes 1048576 | tf_op jit(solution)/shard_map/all_to_all | solution.py:12
  127.3 0.7 reduce.7
  128.2 8.1 %all-to-all-done.6 = f32[8,128,128]{2,1,0:T(8,128)S(1)} async-done(((f32[8,128,128]{2,1,0:T(8,128)}), f32[8,128,128]{2,1,0:T(8,128)S(1)}, u32[]{:S(2)}, u32[]{:S(2)}) %all-to-all-start.6) | async-done | bytes 524320 | tf_op jit(solution)/shard_map/all_to_all | solution.py:12
  137.3 1.5 cholesky.16
  138.8 0.6 compare_reduce_fusion
  139.4 1.2 select_bitcast_fusion
  140.7 1.2 custom-call.7
  141.9 3.9 %convolution_subtract_fusion = f32[16,8192]{1,0:T(8,128)S(1)} fusion(f32[128,16]{0,1:T(8,128)S(1)} %fusion, f32[128,8192]{1,0:T(8,128)} %all-gather.2.cloned.1.call-done, f32[16,1,8192]{2,1,0:T(1,128)S(1)} %all_to_all.38), kind=kOutput, calls=%fused_computation | convolution fusion | flops 201457664 | bytes 5251072 | tf_op jit(solution)/shard_map/dot_general | solution.py:68
  (30 shorter events, 4.4 us)
Async XLA Ops:
  7.2 96.5 %all-gather.2.cloned.1.call-start = ((), (), s32[]{:S(2)}) async-start(), calls=%async_computation.7 | async-start | bytes 4456448 | tf_op jit(solution)/shard_map/all_gather | solution.py:101
  97.1 11.6 %all-to-all-start.4 = ((f32[8,1,256]{2,1,0:T(1,128)}), f32[8,1,256]{2,1,0:T(1,128)S(1)}, u32[]{:S(2)}, u32[]{:S(2)}) async-start(f32[8,1,256]{2,1,0:T(1,128)} %reshape.31), calls=%async_computation.4 | async-start | bytes 16384 | tf_op jit(solution)/shard_map/all_to_all | solution.py:12
  109.4 11.8 %all-to-all-start.5 = ((f32[8,128,16]{1,2,0:T(8,128)}), f32[8,128,16]{1,2,0:T(8,128)S(1)}, u32[]{:S(2)}, u32[]{:S(2)}) async-start(f32[8,128,16]{1,2,0:T(8,128)} %broadcast_in_dim.24), calls=%async_computation.5 | async-start | bytes 131072 | tf_op jit(solution)/shard_map/all_to_all | solution.py:12
  122.0 14.3 %all-to-all-start.6 = ((f32[8,128,128]{2,1,0:T(8,128)}), f32[8,128,128]{2,1,0:T(8,128)S(1)}, u32[]{:S(2)}, u32[]{:S(2)}) async-start(f32[8,128,128]{2,1,0:T(8,128)} %broadcast_in_dim.25), calls=%async_computation.6 | async-start | bytes 1048576 | tf_op jit(solution)/shard_map/all_to_all | solution.py:12
  136.5 10.5 %copy-start = (f32[128,16]{0,1:T(8,128)}, f32[128,16]{0,1:T(8,128)S(1)}, u32[]{:S(2)}) copy-start(f32[128,16]{0,1:T(8,128)S(1)} %fusion) | copy-start | bytes 24580
Sparse Core Ops, SparseCore 0:
  10.2 54.6 all-gather.1
where the time goes:
time: 154 us
  blocking collectives  57 us (37%)
  matrix products  46.5 us (30%)
  starting transfers between devices  16.2 us (11%)
  between operations  14.2 us (9%)
  waiting for transfers between devices  8.8 us (6%)
  other arithmetic  5.71 us (4%)
  local copies, waits for them, and re-layouts  5.4 us (4%)
    all_to_all x3, blocking collectives, from_everyone(): return lax.all_to_all(copies, axis, split_axis=0, concat_axis=0, tiled=True)  45.1 us
    dot_general x4, matrix products, contract(): lax.dot_general(left, right, (((1,), (1,)), ((), ())), precision=lax.Prec...  29.6 us
    dot_general x7, matrix products, matmul(): jnp.dot(left, right, precision=lax.Precision.HIGHEST, preferred_element_t...  16.3 us
    all_to_all x3, starting transfers between devices, from_everyone(): return lax.all_to_all(copies, axis, split_axis=0, concat_axis=0, tiled=True)  16.2 us
    all_to_all x1, blocking collectives, sum_at_owner(): lax.all_to_all(tiles, axis, split_axis=0, concat_axis=0, tiled=True)  11.9 us
    all_to_all x3, waiting for transfers between devices, from_everyone(): return lax.all_to_all(copies, axis, split_axis=0, concat_axis=0, tiled=True)  8.12 us
  transfers between devices with their start and end apart: 4, of which 1 were waited for; matrix products, arithmetic and copies ran while one was open for 30% of the time, Pallas kernels for 0%

commit v1 on v0

v1 whole, which is shorter than its diff:
```python
import functools

import jax
import jax.numpy as jnp
from jax import lax
from jax.experimental import pallas as pl
from jax.experimental.pallas import tpu as pltpu
from jax.sharding import PartitionSpec as P

N = 65536
BS = 16
SIDE = 4
LANES = 128
SUB = 8
MESH = pl.DeviceIdType.MESH
f32, bf16 = jnp.float32, jnp.bfloat16
ROW_BY_ROW = (((1,), (1,)), ((), ()))
ROW_BY_COL = (((1,), (0,)), ((), ()))


def product(left, right, dims):
    return lax.dot_general(left, right, dims, preferred_element_type=f32)


def exact(left, right, dims):
    return lax.dot_general(
        left, right, dims, precision=lax.Precision.HIGHEST, preferred_element_type=f32
    )


def two_terms(value):
    high = value.astype(bf16)
    return high, (value - high.astype(f32)).astype(bf16)


def row_after(row, step):
    x, y = row // SIDE, row % SIDE
    return (x + step // SIDE) % SIDE * SIDE + (y + step % SIDE) % SIDE


def row_before(row, step):
    x, y = row // SIDE, row % SIDE
    return (x + SIDE - step // SIDE) % SIDE * SIDE + (y + SIDE - step % SIDE) % SIDE


def arrive(buffer, sem):
    pltpu.make_async_copy(buffer, buffer, sem).wait()


def kernel(
    rows, cols, a_hbm, basis_hbm, new_ref, coef_ref, factor_ref,
    a_all, a_high, a_low, basis, current, acc, tiles, tiles_in, whole,
    image_out, image_in, corr, corr_in, corr_rows, corr_whole, stat_cols, stat_rows,
    a_sem, basis_sem, cur_send, cur_recv, tile_send, tile_recv, whole_send, whole_recv,
    image_send, image_recv, corr_send, corr_recv, crow_send, crow_recv, call_send, call_recv,
    scol_send, scol_recv, srow_send, srow_recv,
):
    row, col = lax.axis_index("rows"), lax.axis_index("cols")
    width = basis.shape[1]
    prior = basis.shape[0]

    def to_row(source, target, send, recv, peer):
        copy = pltpu.make_async_remote_copy(
            source, target, send, recv, device_id={"rows": peer}, device_id_type=MESH
        )
        copy.start()
        return copy

    def to_col(source, target, send, recv, peer):
        copy = pltpu.make_async_remote_copy(
            source, target, send, recv, device_id={"cols": peer}, device_id_type=MESH
        )
        copy.start()
        return copy

    sent = []
    barrier = pltpu.get_barrier_semaphore()
    for step in range(1, rows):
        pl.semaphore_signal(barrier, inc=1, device_id={"rows": row_after(row, step)}, device_id_type=MESH)
    for step in range(1, cols):
        pl.semaphore_signal(barrier, inc=1, device_id={"cols": (col + step) % cols}, device_id_type=MESH)

    last = basis_hbm.at[pl.ds(prior - BS, BS)]
    pltpu.make_async_copy(last, current.at[row], cur_recv.at[row]).start()
    load_basis = pltpu.make_async_copy(basis_hbm, basis, basis_sem)
    load_basis.start()

    @pl.loop(0, rows)
    def _(step):
        source = row_before(row, step)
        columns = pl.ds(pl.multiple_of(source * width, width), width)
        pltpu.make_async_copy(a_hbm.at[:, columns], a_all.at[source], a_sem.at[source]).start()

    pl.semaphore_wait(barrier, rows + cols - 2)

    for step in range(1, rows):
        peer = row_after(row, step)
        sent.append(to_row(last, current.at[row], cur_send.at[step], cur_recv.at[row], peer))

    load_basis.wait()
    share = prior // cols
    corr[...] = (exact(basis[...], basis[...], ROW_BY_ROW) * (1.0 / N)).reshape(cols, share, prior)
    for step in range(1, cols):
        peer = (col + step) % cols
        sent.append(to_col(corr.at[peer], corr_in.at[col], corr_send.at[step], corr_recv.at[col], peer))

    acc[...] = jnp.zeros_like(acc)

    @pl.loop(0, rows)
    def _(step):
        source = row_before(row, step)
        arrive(a_all.at[source], a_sem.at[source])
        arrive(current.at[source], cur_recv.at[source])
        high, low = two_terms(a_all[source])
        a_high[source] = high
        a_low[source] = low
        cur_high, cur_low = two_terms(current[source])
        both = product(jnp.concatenate([cur_high, cur_low], 0), high, ROW_BY_ROW)
        acc[...] += both[:BS] + both[BS:] + product(cur_high, low, ROW_BY_ROW)

    across = acc.shape[1] // LANES
    for t in range(cols):
        tiles[t] = acc[t // across * SUB : (t // across + 1) * SUB, t % across * LANES : (t % across + 1) * LANES]
    for step in range(1, cols):
        peer = (col + step) % cols
        sent.append(to_col(tiles.at[peer], tiles_in.at[col], tile_send.at[step], tile_recv.at[col], peer))

    total = corr[col]
    for step in range(1, cols):
        source = (col + cols - step) % cols
        arrive(corr_in.at[source], corr_recv.at[source])
        total += corr_in[source]
    corr_rows[row] = total
    for step in range(1, rows):
        peer = row_after(row, step)
        sent.append(to_row(corr_rows.at[row], corr_rows.at[row], crow_send.at[step], crow_recv.at[row], peer))

    total = tiles[col]
    for step in range(1, cols):
        source = (col + cols - step) % cols
        arrive(tiles_in.at[source], tile_recv.at[source])
        total += tiles_in[source]
    whole[col] = total
    for step in range(1, cols):
        peer = (col + step) % cols
        sent.append(to_col(whole.at[col], whole.at[col], whole_send.at[step], whole_recv.at[col], peer))
    for step in range(1, cols):
        source = (col + cols - step) % cols
        arrive(whole.at[source], whole_recv.at[source])
    projected = jnp.concatenate(
        [jnp.concatenate([whole[t] for t in range(top * across, (top + 1) * across)], 1) for top in range(BS // SUB)], 0
    )

    pro_high, pro_low = two_terms(projected)
    pro_both = jnp.concatenate([pro_high, pro_low], 0)

    def block(peer):
        both = product(pro_both, a_high[peer], ROW_BY_COL)
        return both[:BS] + both[BS:] + product(pro_high, a_low[peer], ROW_BY_COL)

    @pl.loop(1, rows)
    def _(step):
        peer = row_after(row, step)
        image_out[peer] = block(peer)
        to_row(image_out.at[peer], image_in.at[row], image_send.at[step], image_recv.at[row], peer)

    image = block(row)

    total = jnp.zeros_like(corr_rows[0])
    for source in range(rows):
        @pl.when(source != row)
        def _():
            arrive(corr_rows.at[source], crow_recv.at[source])
        total += corr_rows[source]
    corr_whole[col] = total
    for step in range(1, cols):
        peer = (col + step) % cols
        sent.append(to_col(corr_whole.at[col], corr_whole.at[col], call_send.at[step], call_recv.at[col], peer))

    for step in range(1, rows):
        source = row_before(row, step)
        arrive(image_in.at[source], image_recv.at[source])
        image += image_in[source]

    own = basis[...]
    pairs = exact(image, jnp.concatenate([own, image], 0), ROW_BY_ROW) * (1.0 / N)
    stat_cols[col, :BS] = pairs[:, :prior]
    stat_cols[col, BS:] = jnp.concatenate([pairs[:, prior:], jnp.zeros((BS, prior - BS), f32)], 1)
    for step in range(1, cols):
        peer = (col + step) % cols
        sent.append(to_col(stat_cols.at[col], stat_cols.at[col], scol_send.at[step], scol_recv.at[col], peer))

    for step in range(1, cols):
        source = (col + cols - step) % cols
        arrive(corr_whole.at[source], call_recv.at[source])
    correlation = corr_whole[...].reshape(prior, prior)
    at = lax.broadcasted_iota(jnp.int32, (prior, prior), 0)
    double = jnp.where(at == lax.broadcasted_iota(jnp.int32, (prior, prior), 1), 2.0, 0.0) - correlation
    inner = 2.0 * double - exact(exact(double, correlation, ROW_BY_COL), double, ROW_BY_COL)

    for step in range(1, cols):
        source = (col + cols - step) % cols
        arrive(stat_cols.at[source], scol_recv.at[source])
    total = stat_cols[0]
    for source in range(1, cols):
        total += stat_cols[source]
    stat_rows[row] = total
    for step in range(1, rows):
        peer = row_after(row, step)
        sent.append(to_row(stat_rows.at[row], stat_rows.at[row], srow_send.at[step], srow_recv.at[row], peer))
    for step in range(1, rows):
        source = row_before(row, step)
        arrive(stat_rows.at[source], srow_recv.at[source])
    total = stat_rows[0]
    for source in range(1, rows):
        total += stat_rows[source]

    cross, self_gram = total[:BS], total[BS:, :BS]
    coeffs = exact(cross, double, ROW_BY_ROW)
    gram = self_gram - exact(exact(cross, inner, ROW_BY_ROW), cross, ROW_BY_ROW)
    image -= exact(coeffs, own, ROW_BY_COL)
    coef_ref[...] = coeffs

    line = lax.broadcasted_iota(jnp.int32, (BS, BS), 0)
    lane = lax.broadcasted_iota(jnp.int32, (BS, BS), 1)
    below = lax.broadcasted_iota(jnp.int32, (BS, 1), 0)
    factor = jnp.zeros((BS, BS), f32)
    for j in range(BS):
        column = gram[:, j : j + 1]
        scale = 1.0 / jnp.sqrt(column[j : j + 1])
        column = column * scale
        gram_line = gram[j : j + 1] * scale
        image_line = image[j : j + 1] * scale
        factor = jnp.where((lane == j) & (line >= j), column, factor)
        part = jnp.where(below > j, column, 0.0)
        gram = gram - part * gram_line
        image = jnp.where(below == j, image_line, image - part * image_line)
    new_ref[...] = image
    factor_ref[...] = factor

    for copy in sent:
        copy.wait_send()

    @pl.loop(1, rows)
    def _(step):
        arrive(image_out.at[row_after(row, step)], image_send.at[step])


def local(rows, cols, projection, basis):
    rays, columns = projection.shape
    prior, width = basis.shape
    dma = pltpu.SemaphoreType.DMA
    call = pl.pallas_call(
        functools.partial(kernel, rows, cols),
        out_shape=(
            jax.ShapeDtypeStruct((BS, width), f32),
            jax.ShapeDtypeStruct((BS, prior), f32),
            jax.ShapeDtypeStruct((BS, BS), f32),
        ),
        in_specs=[pl.BlockSpec(memory_space=pltpu.HBM)] * 2,
        out_specs=[pl.BlockSpec(memory_space=pltpu.VMEM)] * 3,
        scratch_shapes=[
            pltpu.VMEM((rows, rays, width), f32),
            pltpu.VMEM((rows, rays, width), bf16),
            pltpu.VMEM((rows, rays, width), bf16),
            pltpu.VMEM((prior, width), f32),
            pltpu.VMEM((rows, BS, width), f32),
            pltpu.VMEM((BS, rays), f32),
            pltpu.VMEM((cols, SUB, LANES), f32),
            pltpu.VMEM((cols, SUB, LANES), f32),
            pltpu.VMEM((cols, SUB, LANES), f32),
            pltpu.VMEM((rows, BS, width), f32),
            pltpu.VMEM((rows, BS, width), f32),
            pltpu.VMEM((cols, prior // cols, prior), f32),
            pltpu.VMEM((cols, prior // cols, prior), f32),
            pltpu.VMEM((rows, prior // cols, prior), f32),
            pltpu.VMEM((cols, prior // cols, prior), f32),
            pltpu.VMEM((cols, 2 * BS, prior), f32),
            pltpu.VMEM((rows, 2 * BS, prior), f32),
            dma((rows,)), dma,
            dma((rows,)), dma((rows,)),
            dma((cols,)), dma((cols,)), dma((cols,)), dma((cols,)),
            dma((rows,)), dma((rows,)),
            dma((cols,)), dma((cols,)), dma((rows,)), dma((rows,)), dma((cols,)), dma((cols,)),
            dma((cols,)), dma((cols,)), dma((rows,)), dma((rows,)),
        ],
        compiler_params=pltpu.CompilerParams(
            collective_id=0, has_side_effects=True, vmem_limit_bytes=48 << 20
        ),
    )
    new_block, coefficients, factor = call(projection, basis)
    return new_block, coefficients.T, factor


def solution(mesh):
    placed = (P("rows", "cols"), P(None, ("cols", "rows")))
    return jax.shard_map(
        functools.partial(local, mesh.shape["rows"], mesh.shape["cols"]),
        mesh=mesh,
        in_specs=placed,
        out_specs=(P(None, ("cols", "rows")), P(), P()),
        check_vma=False,
    )
```

time: 154 us -> 57.5 us (0.37)
  blocking collectives: 57 us -> 0 us
  Pallas kernels: 0 us -> 53.9 us
  matrix products: 46.5 us -> 0 us
  starting transfers between devices: 16.2 us -> 0 us
  between operations: 14.2 us -> 0.65 us
  waiting for transfers between devices: 8.8 us -> 0 us
  other arithmetic: 5.71 us -> 0 us
  local copies, waits for them, and re-layouts: 5.4 us -> 2.76 us
    all_to_all x4 -> x0, blocking collectives: 57 us -> none  [the longest x3 45.1 us: from_everyone(): return lax.all_to_all(copies, axis, split_axis=0, concat_axis=0, tiled=True)]
    pallas_call x0 -> x1, Pallas kernels: none -> 53.9 us  [local(): new_block, coefficients, factor = call(projection, basis)]
    dot_general x11 -> x0, matrix products: 45.9 us -> none  [the longest x4 29.6 us: contract(): lax.dot_general(left, right, (((1,), (1,)), ((), ())), precision=lax.Prec...]
    all_to_all x3 -> x0, starting transfers between devices: 16.2 us -> none  [from_everyone(): return lax.all_to_all(copies, axis, split_axis=0, concat_axis=0, tiled=True)]
    all_to_all x3 -> x0, waiting for transfers between devices: 8.12 us -> none  [from_everyone(): return lax.all_to_all(copies, axis, split_axis=0, concat_axis=0, tiled=True)]
    another operation x5 -> x0, other arithmetic: 4.61 us -> none  [the longest x2 2.47 us: orthogonalize(): new_block = jax.scipy.linalg.solve_triangular(factor, image_two, lower=True)]
    broadcast_in_dim x6 -> x0, local copies, waits for them, and re-layouts: 1.95 us -> none  [from_everyone(): copies = jnp.broadcast_to(array, (lax.axis_size(axis), *array.shape))]
    unnamed x4 -> x5, local copies, waits for them, and re-layouts: 0.82 us -> 2.76 us
  transfers between devices with their start and end apart: 4 -> 0, of which waited for: 1 -> 0; matrix products, arithmetic and copies ran while one was open for 30% -> 0% of each run, Pallas kernels for 0% -> 0%
where the time goes in v1:
time: 57.5 us; the launch traced here: 57.3 us
  Pallas kernels  53.9 us (94%)
  local copies, waits for them, and re-layouts  2.76 us (5%)
  between operations  0.65 us (1%)
    pallas_call x1, Pallas kernels, local(): new_block, coefficients, factor = call(projection, basis)  53.9 us
    unnamed x5, local copies, waits for them, and re-layouts  2.76 us

profile of v1, /device:TPU:1, one launch (start us, length us, event | category | flops | bytes accessed | tf_op | source)
XLA Modules:
  0.0 57.3 jit_solution(17875848720188613847)
XLA Ops:
  0.6 0.0 copy-start
  0.6 0.9 %copy-done = f32[128,512]{1,0:T(8,128)S(1)} copy-done((f32[128,512]{1,0:T(8,128)S(1)}, f32[128,512]{1,0:T(8,128)}, u32[]{:S(2)}) %copy-start) | copy-done | bytes 262168
  1.6 53.9 %shard_map.49 = (f32[16,512]{1,0:T(8,128)S(1)}, f32[16,128]{1,0:T(8,128)S(1)}, f32[16,16]{1,0:T(8,128)S(1)}) custom-call(f32[512,8192]{1,0:T(8,128)} %a_hbm.1, f32[128,512]{1,0:T(8,128)S(1)} %copy-done), custom_call_target="tpu_custom_call" | custom-call | tf_op jit(solution)/shard_map/pallas_call | solution.py:291
  55.5 0.6 %copy.8 = f32[16,512]{1,0:T(8,128)} copy(f32[16,512]{1,0:T(8,128)S(1)} %get-tuple-element.12) | data formatting | bytes 65536
  56.1 0.6 %copy.9 = f32[128,16]{0,1:T(8,128)} copy(f32[128,16]{0,1:T(8,128)S(1)} %bitcast.1) | data formatting | bytes 16384
  56.7 0.6 %copy.10 = f32[16,16]{1,0:T(8,128)} copy(f32[16,16]{1,0:T(8,128)S(1)} %get-tuple-element.14) | data formatting | bytes 2048
Async XLA Ops:
  0.6 1.0 %copy-start = (f32[128,512]{1,0:T(8,128)S(1)}, f32[128,512]{1,0:T(8,128)}, u32[]{:S(2)}) copy-start(f32[128,512]{1,0:T(8,128)} %basis_hbm.1) | copy-start | bytes 786436

commit v2 on v1

--- a/solution.py
+++ b/solution.py
@@ -9,10 +9,14 @@
 
 N = 65536
 BS = 16
+DEPTH = 6
+EARLY = 4
 SIDE = 4
-LANES = 128
-SUB = 8
 MESH = pl.DeviceIdType.MESH
+BOTH_AXES = [5, 6, 7, 9, 10, 11, 13, 14, 15]
+ONE_AXIS = [1, 2, 3, 4, 8, 12]
+FAR_FIRST = BOTH_AXES + ONE_AXIS
+NEAR_FIRST = ONE_AXIS + BOTH_AXES
 f32, bf16 = jnp.float32, jnp.bfloat16
 ROW_BY_ROW = (((1,), (1,)), ((), ()))
 ROW_BY_COL = (((1,), (0,)), ((), ()))
@@ -43,15 +47,24 @@
     return (x + SIDE - step // SIDE) % SIDE * SIDE + (y + SIDE - step % SIDE) % SIDE
 
 
+def near_first(step):
+    both = step - 7
+    return jnp.where(step < 4, step, jnp.where(step < 7, 4 * (step - 3), 5 + both // 3 * 4 + both % 3))
+
+
+def far_first(step):
+    return near_first((step + 5) % 15 + 1)
+
+
 def arrive(buffer, sem):
     pltpu.make_async_copy(buffer, buffer, sem).wait()
 
 
 def kernel(
     rows, cols, a_hbm, basis_hbm, new_ref, coef_ref, factor_ref,
-    a_all, a_high, a_low, basis, current, acc, tiles, tiles_in, whole,
+    a_stage, a_high, a_low, a_high_t, a_low_t, basis, current, acc, parts,
     image_out, image_in, corr, corr_in, corr_rows, corr_whole, stat_cols, stat_rows,
-    a_sem, basis_sem, cur_send, cur_recv, tile_send, tile_recv, whole_send, whole_recv,
+    a_sem, basis_sem, cur_send, cur_recv, part_send, part_recv,
     image_send, image_recv, corr_send, corr_recv, crow_send, crow_recv, call_send, call_recv,
     scol_send, scol_recv, srow_send, srow_recv,
 ):
@@ -75,7 +88,7 @@
 
     sent = []
     barrier = pltpu.get_barrier_semaphore()
-    for step in range(1, rows):
+    for step in FAR_FIRST:
         pl.semaphore_signal(barrier, inc=1, device_id={"rows": row_after(row, step)}, device_id_type=MESH)
     for step in range(1, cols):
         pl.semaphore_signal(barrier, inc=1, device_id={"cols": (col + step) % cols}, device_id_type=MESH)
@@ -85,17 +98,41 @@
     load_basis = pltpu.make_async_copy(basis_hbm, basis, basis_sem)
     load_basis.start()
 
-    @pl.loop(0, rows)
-    def _(step):
-        source = row_before(row, step)
-        columns = pl.ds(pl.multiple_of(source * width, width), width)
-        pltpu.make_async_copy(a_hbm.at[:, columns], a_all.at[source], a_sem.at[source]).start()
-
+    depth = a_stage.shape[0]
+
+    def fetch(block):
+        columns = pl.ds(pl.multiple_of(block * width, width), width)
+        slot = block % depth
+        return pltpu.make_async_copy(a_hbm.at[:, columns], a_stage.at[slot], a_sem.at[slot])
+
+    def prepare(block):
+        fetch(block).wait()
+        plain = a_stage[block % depth]
+        turned = plain.T
+        high, low = two_terms(plain)
+        a_high[block] = high
+        a_low[block] = low
+        high, low = two_terms(turned)
+        a_high_t[block] = high
+        a_low_t[block] = low
+
+        @pl.when(block + depth < rows)
+        def _():
+            fetch(block + depth).start()
+
+    for block in range(depth):
+        fetch(block).start()
+
+    @pl.loop(0, EARLY)
+    def _(block):
+        prepare(block)
+
+    arrive(current.at[row], cur_recv.at[row])
     pl.semaphore_wait(barrier, rows + cols - 2)
 
-    for step in range(1, rows):
+    for step in FAR_FIRST:
         peer = row_after(row, step)
-        sent.append(to_row(last, current.at[row], cur_send.at[step], cur_recv.at[row], peer))
+        sent.append(to_row(current.at[row], current.at[row], cur_send.at[step], cur_recv.at[row], peer))
 
     load_basis.wait()
     share = prior // cols
@@ -104,26 +141,27 @@
         peer = (col + step) % cols
         sent.append(to_col(corr.at[peer], corr_in.at[col], corr_send.at[step], corr_recv.at[col], peer))
 
-    acc[...] = jnp.zeros_like(acc)
-
-    @pl.loop(0, rows)
+    @pl.loop(EARLY, rows)
+    def _(block):
+        prepare(block)
+
+    def rays(source):
+        cur_high, cur_low = two_terms(current[source])
+        both = product(jnp.concatenate([cur_high, cur_low], 0), a_high_t[source], ROW_BY_COL)
+        return both[:BS] + both[BS:] + product(cur_high, a_low_t[source], ROW_BY_COL)
+
+    acc[...] = rays(row)
+
+    @pl.loop(1, rows)
     def _(step):
-        source = row_before(row, step)
-        arrive(a_all.at[source], a_sem.at[source])
+        source = row_before(row, near_first(step))
         arrive(current.at[source], cur_recv.at[source])
-        high, low = two_terms(a_all[source])
-        a_high[source] = high
-        a_low[source] = low
-        cur_high, cur_low = two_terms(current[source])
-        both = product(jnp.concatenate([cur_high, cur_low], 0), high, ROW_BY_ROW)
-        acc[...] += both[:BS] + both[BS:] + product(cur_high, low, ROW_BY_ROW)
-
-    across = acc.shape[1] // LANES
-    for t in range(cols):
-        tiles[t] = acc[t // across * SUB : (t // across + 1) * SUB, t % across * LANES : (t % across + 1) * LANES]
+        acc[...] += rays(source)
+
+    parts[col] = acc[...]
     for step in range(1, cols):
         peer = (col + step) % cols
-        sent.append(to_col(tiles.at[peer], tiles_in.at[col], tile_send.at[step], tile_recv.at[col], peer))
+        sent.append(to_col(parts.at[col], parts.at[col], part_send.at[step], part_recv.at[col], peer))
 
     total = corr[col]
     for step in range(1, cols):
@@ -135,21 +173,12 @@
         peer = row_after(row, step)
         sent.append(to_row(corr_rows.at[row], corr_rows.at[row], crow_send.at[step], crow_recv.at[row], peer))
 
-    total = tiles[col]
     for step in range(1, cols):
         source = (col + cols - step) % cols
-        arrive(tiles_in.at[source], tile_recv.at[source])
-        total += tiles_in[source]
-    whole[col] = total
-    for step in range(1, cols):
-        peer = (col + step) % cols
-        sent.append(to_col(whole.at[col], whole.at[col], whole_send.at[step], whole_recv.at[col], peer))
-    for step in range(1, cols):
-        source = (col + cols - step) % cols
-        arrive(whole.at[source], whole_recv.at[source])
-    projected = jnp.concatenate(
-        [jnp.concatenate([whole[t] for t in range(top * across, (top + 1) * across)], 1) for top in range(BS // SUB)], 0
-    )
+        arrive(parts.at[source], part_recv.at[source])
+    projected = parts[0]
+    for source in range(1, cols):
+        projected += parts[source]
 
     pro_high, pro_low = two_terms(projected)
     pro_both = jnp.concatenate([pro_high, pro_low], 0)
@@ -160,7 +189,7 @@
 
     @pl.loop(1, rows)
     def _(step):
-        peer = row_after(row, step)
+        peer = row_after(row, far_first(step))
         image_out[peer] = block(peer)
         to_row(image_out.at[peer], image_in.at[row], image_send.at[step], image_recv.at[row], peer)
 
@@ -205,7 +234,7 @@
     for source in range(1, cols):
         total += stat_cols[source]
     stat_rows[row] = total
-    for step in range(1, rows):
+    for step in FAR_FIRST:
         peer = row_after(row, step)
         sent.append(to_row(stat_rows.at[row], stat_rows.at[row], srow_send.at[step], srow_recv.at[row], peer))
     for step in range(1, rows):
@@ -260,15 +289,15 @@
         in_specs=[pl.BlockSpec(memory_space=pltpu.HBM)] * 2,
         out_specs=[pl.BlockSpec(memory_space=pltpu.VMEM)] * 3,
         scratch_shapes=[
-            pltpu.VMEM((rows, rays, width), f32),
+            pltpu.VMEM((DEPTH, rays, width), f32),
             pltpu.VMEM((rows, rays, width), bf16),
             pltpu.VMEM((rows, rays, width), bf16),
+            pltpu.VMEM((rows, width, rays), bf16),
+            pltpu.VMEM((rows, width, rays), bf16),
             pltpu.VMEM((prior, width), f32),
             pltpu.VMEM((rows, BS, width), f32),
             pltpu.VMEM((BS, rays), f32),
-            pltpu.VMEM((cols, SUB, LANES), f32),
-            pltpu.VMEM((cols, SUB, LANES), f32),
-            pltpu.VMEM((cols, SUB, LANES), f32),
+            pltpu.VMEM((cols, BS, rays), f32),
             pltpu.VMEM((rows, BS, width), f32),
             pltpu.VMEM((rows, BS, width), f32),
             pltpu.VMEM((cols, prior // cols, prior), f32),
@@ -277,9 +306,9 @@
             pltpu.VMEM((cols, prior // cols, prior), f32),
             pltpu.VMEM((cols, 2 * BS, prior), f32),
             pltpu.VMEM((rows, 2 * BS, prior), f32),
-            dma((rows,)), dma,
+            dma((DEPTH,)), dma,
             dma((rows,)), dma((rows,)),
-            dma((cols,)), dma((cols,)), dma((cols,)), dma((cols,)),
+            dma((cols,)), dma((cols,)),
             dma((rows,)), dma((rows,)),
             dma((cols,)), dma((cols,)), dma((rows,)), dma((rows,)), dma((cols,)), dma((cols,)),
             dma((cols,)), dma((cols,)), dma((rows,)), dma((rows,)),

time: 57.5 us -> 52.4 us (0.911)
  Pallas kernels: 53.9 us -> 48.8 us
    pallas_call x1, Pallas kernels: 53.9 us -> 48.8 us  [local(): new_block, coefficients, factor = call(projection, basis)]
where the time goes in v2:
time: 52.4 us; the launch traced here: 52.2 us
  Pallas kernels  48.8 us (93%)
  local copies, waits for them, and re-layouts  2.76 us (5%)
  between operations  0.65 us (1%)
    pallas_call x1, Pallas kernels, local(): new_block, coefficients, factor = call(projection, basis)  48.8 us
    unnamed x5, local copies, waits for them, and re-layouts  2.76 us

profile of v2, /device:TPU:1, one launch (start us, length us, event | category | flops | bytes accessed | tf_op | source)
XLA Modules:
  0.0 52.2 jit_solution(15173493873047909719)
XLA Ops:
  0.6 0.0 copy-start
  0.6 0.9 %copy-done = f32[128,512]{1,0:T(8,128)S(1)} copy-done((f32[128,512]{1,0:T(8,128)S(1)}, f32[128,512]{1,0:T(8,128)}, u32[]{:S(2)}) %copy-start) | copy-done | bytes 262168
  1.6 48.8 %shard_map.49 = (f32[16,512]{1,0:T(8,128)S(1)}, f32[16,128]{1,0:T(8,128)S(1)}, f32[16,16]{1,0:T(8,128)S(1)}) custom-call(f32[512,8192]{1,0:T(8,128)} %a_hbm.1, f32[128,512]{1,0:T(8,128)S(1)} %copy-done), custom_call_target="tpu_custom_call" | custom-call | tf_op jit(solution)/shard_map/pallas_call | solution.py:320
  50.4 0.6 %copy.8 = f32[16,512]{1,0:T(8,128)} copy(f32[16,512]{1,0:T(8,128)S(1)} %get-tuple-element.12) | data formatting | bytes 65536
  51.0 0.6 %copy.9 = f32[128,16]{0,1:T(8,128)} copy(f32[128,16]{0,1:T(8,128)S(1)} %bitcast.1) | data formatting | bytes 16384
  51.6 0.6 %copy.10 = f32[16,16]{1,0:T(8,128)} copy(f32[16,16]{1,0:T(8,128)S(1)} %get-tuple-element.14) | data formatting | bytes 2048
Async XLA Ops:
  0.6 1.0 %copy-start = (f32[128,512]{1,0:T(8,128)S(1)}, f32[128,512]{1,0:T(8,128)}, u32[]{:S(2)}) copy-start(f32[128,512]{1,0:T(8,128)} %basis_hbm.1) | copy-start | bytes 786436

commit v3 on v2

--- a/solution.py
+++ b/solution.py
@@ -11,12 +11,10 @@
 BS = 16
 DEPTH = 6
 EARLY = 4
+LAST = 6
 SIDE = 4
 MESH = pl.DeviceIdType.MESH
-BOTH_AXES = [5, 6, 7, 9, 10, 11, 13, 14, 15]
-ONE_AXIS = [1, 2, 3, 4, 8, 12]
-FAR_FIRST = BOTH_AXES + ONE_AXIS
-NEAR_FIRST = ONE_AXIS + BOTH_AXES
+FAR_FIRST = [10, 6, 9, 14, 11, 5, 7, 13, 15, 8, 2, 1, 3, 4, 12]
 f32, bf16 = jnp.float32, jnp.bfloat16
 ROW_BY_ROW = (((1,), (1,)), ((), ()))
 ROW_BY_COL = (((1,), (0,)), ((), ()))
@@ -47,13 +45,11 @@
     return (x + SIDE - step // SIDE) % SIDE * SIDE + (y + SIDE - step % SIDE) % SIDE
 
 
-def near_first(step):
-    both = step - 7
-    return jnp.where(step < 4, step, jnp.where(step < 7, 4 * (step - 3), 5 + both // 3 * 4 + both % 3))
-
-
 def far_first(step):
-    return near_first((step + 5) % 15 + 1)
+    place = 0
+    for k, at in enumerate(FAR_FIRST):
+        place = jnp.where(step == k + 1, at, place)
+    return place
 
 
 def arrive(buffer, sem):
@@ -63,10 +59,10 @@
 def kernel(
     rows, cols, a_hbm, basis_hbm, new_ref, coef_ref, factor_ref,
     a_stage, a_high, a_low, a_high_t, a_low_t, basis, current, acc, parts,
-    image_out, image_in, corr, corr_in, corr_rows, corr_whole, stat_cols, stat_rows,
+    image_out, image_in, corr, corr_in, corr_rows, corr_whole, stat_cols, stat_rows, squares,
     a_sem, basis_sem, cur_send, cur_recv, part_send, part_recv,
     image_send, image_recv, corr_send, corr_recv, crow_send, crow_recv, call_send, call_recv,
-    scol_send, scol_recv, srow_send, srow_recv,
+    scol_send, scol_recv, srow_send, srow_recv, square_send, square_recv,
 ):
     row, col = lax.axis_index("rows"), lax.axis_index("cols")
     width = basis.shape[1]
@@ -145,23 +141,33 @@
     def _(block):
         prepare(block)
 
-    def rays(source):
+    half = acc.shape[1] // 2
+
+    def rays(source, columns):
         cur_high, cur_low = two_terms(current[source])
-        both = product(jnp.concatenate([cur_high, cur_low], 0), a_high_t[source], ROW_BY_COL)
-        return both[:BS] + both[BS:] + product(cur_high, a_low_t[source], ROW_BY_COL)
-
-    acc[...] = rays(row)
-
-    @pl.loop(1, rows)
+        both = product(jnp.concatenate([cur_high, cur_low], 0), a_high_t[source, :, columns], ROW_BY_COL)
+        return both[:BS] + both[BS:] + product(cur_high, a_low_t[source, :, columns], ROW_BY_COL)
+
+    acc[...] = rays(row, slice(None))
+
+    @pl.loop(1, rows - LAST)
     def _(step):
-        source = row_before(row, near_first(step))
+        source = row_before(row, far_first(step))
         arrive(current.at[source], cur_recv.at[source])
-        acc[...] += rays(source)
-
-    parts[col] = acc[...]
-    for step in range(1, cols):
-        peer = (col + step) % cols
-        sent.append(to_col(parts.at[col], parts.at[col], part_send.at[step], part_recv.at[col], peer))
+        acc[...] += rays(source, slice(None))
+
+    for part in range(2):
+        columns = slice(part * half, (part + 1) * half)
+        total = acc[:, columns]
+        for step in FAR_FIRST[rows - LAST - 1 :]:
+            source = row_before(row, step)
+            if part == 0:
+                arrive(current.at[source], cur_recv.at[source])
+            total += rays(source, columns)
+        parts[part, col] = total
+        for step in range(1, cols):
+            peer = (col + step) % cols
+            sent.append(to_col(parts.at[part, col], parts.at[part, col], part_send.at[part, step], part_recv.at[part, col], peer))
 
     total = corr[col]
     for step in range(1, cols):
@@ -173,12 +179,16 @@
         peer = row_after(row, step)
         sent.append(to_row(corr_rows.at[row], corr_rows.at[row], crow_send.at[step], crow_recv.at[row], peer))
 
-    for step in range(1, cols):
-        source = (col + cols - step) % cols
-        arrive(parts.at[source], part_recv.at[source])
-    projected = parts[0]
-    for source in range(1, cols):
-        projected += parts[source]
+    halves = []
+    for part in range(2):
+        for step in range(1, cols):
+            source = (col + cols - step) % cols
+            arrive(parts.at[part, source], part_recv.at[part, source])
+        total = parts[part, 0]
+        for source in range(1, cols):
+            total += parts[part, source]
+        halves.append(total)
+    projected = jnp.concatenate(halves, 1)
 
     pro_high, pro_low = two_terms(projected)
     pro_both = jnp.concatenate([pro_high, pro_low], 0)
@@ -212,12 +222,16 @@
         image += image_in[source]
 
     own = basis[...]
-    pairs = exact(image, jnp.concatenate([own, image], 0), ROW_BY_ROW) * (1.0 / N)
-    stat_cols[col, :BS] = pairs[:, :prior]
-    stat_cols[col, BS:] = jnp.concatenate([pairs[:, prior:], jnp.zeros((BS, prior - BS), f32)], 1)
+    stat_cols[col] = exact(image, jnp.concatenate([own[: prior - BS], image], 0), ROW_BY_ROW) * (1.0 / N)
     for step in range(1, cols):
         peer = (col + step) % cols
         sent.append(to_col(stat_cols.at[col], stat_cols.at[col], scol_send.at[step], scol_recv.at[col], peer))
+
+    square = exact(projected, projected, ROW_BY_ROW) * (1.0 / N)
+    squares[row] = jnp.concatenate([square, jnp.zeros((BS, prior - BS), f32)], 1)
+    for step in FAR_FIRST:
+        peer = row_after(row, step)
+        sent.append(to_row(squares.at[row], squares.at[row], square_send.at[step], square_recv.at[row], peer))
 
     for step in range(1, cols):
         source = (col + cols - step) % cols
@@ -240,11 +254,16 @@
     for step in range(1, rows):
         source = row_before(row, step)
         arrive(stat_rows.at[source], srow_recv.at[source])
+        arrive(squares.at[source], square_recv.at[source])
     total = stat_rows[0]
     for source in range(1, rows):
         total += stat_rows[source]
 
-    cross, self_gram = total[:BS], total[BS:, :BS]
+    square = squares[0]
+    for source in range(1, rows):
+        square += squares[source]
+    cross = jnp.concatenate([total[:, : prior - BS], square[:, :BS]], 1)
+    self_gram = total[:, prior - BS :]
     coeffs = exact(cross, double, ROW_BY_ROW)
     gram = self_gram - exact(exact(cross, inner, ROW_BY_ROW), cross, ROW_BY_ROW)
     image -= exact(coeffs, own, ROW_BY_COL)
@@ -297,24 +316,25 @@
             pltpu.VMEM((prior, width), f32),
             pltpu.VMEM((rows, BS, width), f32),
             pltpu.VMEM((BS, rays), f32),
-            pltpu.VMEM((cols, BS, rays), f32),
+            pltpu.VMEM((2, cols, BS, rays // 2), f32),
             pltpu.VMEM((rows, BS, width), f32),
             pltpu.VMEM((rows, BS, width), f32),
             pltpu.VMEM((cols, prior // cols, prior), f32),
             pltpu.VMEM((cols, prior // cols, prior), f32),
             pltpu.VMEM((rows, prior // cols, prior), f32),
             pltpu.VMEM((cols, prior // cols, prior), f32),
-            pltpu.VMEM((cols, 2 * BS, prior), f32),
-            pltpu.VMEM((rows, 2 * BS, prior), f32),
+            pltpu.VMEM((cols, BS, prior), f32),
+            pltpu.VMEM((rows, BS, prior), f32),
+            pltpu.VMEM((rows, BS, prior), f32),
             dma((DEPTH,)), dma,
             dma((rows,)), dma((rows,)),
-            dma((cols,)), dma((cols,)),
+            dma((2, cols)), dma((2, cols)),
             dma((rows,)), dma((rows,)),
             dma((cols,)), dma((cols,)), dma((rows,)), dma((rows,)), dma((cols,)), dma((cols,)),
-            dma((cols,)), dma((cols,)), dma((rows,)), dma((rows,)),
+            dma((cols,)), dma((cols,)), dma((rows,)), dma((rows,)), dma((rows,)), dma((rows,)),
         ],
         compiler_params=pltpu.CompilerParams(
-            collective_id=0, has_side_effects=True, vmem_limit_bytes=48 << 20
+            collective_id=0, has_side_effects=True, vmem_limit_bytes=55040 << 10
         ),
     )
     new_block, coefficients, factor = call(projection, basis)

time: 52.4 us -> 48 us (0.916)
  Pallas kernels: 48.8 us -> 45.4 us
  local copies, waits for them, and re-layouts: 2.76 us -> 1.81 us
    pallas_call x1, Pallas kernels: 48.8 us -> 45.4 us  [local(): new_block, coefficients, factor = call(projection, basis)]
    unnamed x5 -> x3, local copies, waits for them, and re-layouts: 2.76 us -> 1.81 us
where the time goes in v3:
time: 48 us; the launch traced here: 47.9 us
  Pallas kernels  45.4 us (95%)
  local copies, waits for them, and re-layouts  1.81 us (4%)
  between operations  0.64 us (1%)
    pallas_call x1, Pallas kernels, local(): new_block, coefficients, factor = call(projection, basis)  45.4 us
    unnamed x3, local copies, waits for them, and re-layouts  1.81 us

profile of v3, /device:TPU:1, one launch (start us, length us, event | category | flops | bytes accessed | tf_op | source)
XLA Modules:
  0.0 47.9 jit_solution(12308600004669613373)
XLA Ops:
  0.6 45.4 %shard_map.49 = (f32[16,512]{1,0:T(8,128)S(1)}, f32[16,128]{1,0:T(8,128)S(1)}, f32[16,16]{1,0:T(8,128)S(1)}) custom-call(f32[512,8192]{1,0:T(8,128)} %a_hbm.1, f32[128,512]{1,0:T(8,128)} %basis_hbm.1), custom_call_target="tpu_custom_call" | custom-call | tf_op jit(solution)/shard_map/pallas_call | solution.py:340
  46.1 0.6 %copy.8 = f32[16,512]{1,0:T(8,128)} copy(f32[16,512]{1,0:T(8,128)S(1)} %get-tuple-element.12) | data formatting | bytes 65536
  46.7 0.6 %copy.9 = f32[128,16]{0,1:T(8,128)} copy(f32[128,16]{0,1:T(8,128)S(1)} %bitcast.1) | data formatting | bytes 16384
  47.3 0.6 %copy.10 = f32[16,16]{1,0:T(8,128)} copy(f32[16,16]{1,0:T(8,128)S(1)} %get-tuple-element.14) | data formatting | bytes 2048

commit v4 on v3

--- a/solution.py
+++ b/solution.py
@@ -10,8 +10,10 @@
 N = 65536
 BS = 16
 DEPTH = 6
-EARLY = 4
+EARLY = 3
 LAST = 6
+GROUP = 3
+GROUP_OUT = 2
 SIDE = 4
 MESH = pl.DeviceIdType.MESH
 FAR_FIRST = [10, 6, 9, 14, 11, 5, 7, 13, 15, 8, 2, 1, 3, 4, 12]
@@ -150,24 +152,31 @@
 
     acc[...] = rays(row, slice(None))
 
-    @pl.loop(1, rows - LAST)
-    def _(step):
-        source = row_before(row, far_first(step))
+    @pl.loop(0, (rows - 1 - LAST) // GROUP)
+    def _(group):
+        sources = [row_before(row, far_first(group * GROUP + k + 1)) for k in range(GROUP)]
+        for source in sources:
+            arrive(current.at[source], cur_recv.at[source])
+        total = acc[...]
+        for source in sources:
+            total += rays(source, slice(None))
+        acc[...] = total
+
+    sources = [row_before(row, step) for step in FAR_FIRST[rows - LAST - 1 :]]
+    for source in sources:
         arrive(current.at[source], cur_recv.at[source])
-        acc[...] += rays(source, slice(None))
-
-    for part in range(2):
-        columns = slice(part * half, (part + 1) * half)
+
+    @pl.loop(0, 2)
+    def _(part):
+        columns = pl.ds(pl.multiple_of(part * half, half), half)
         total = acc[:, columns]
-        for step in FAR_FIRST[rows - LAST - 1 :]:
-            source = row_before(row, step)
-            if part == 0:
-                arrive(current.at[source], cur_recv.at[source])
+        for source in sources:
             total += rays(source, columns)
         parts[part, col] = total
-        for step in range(1, cols):
-            peer = (col + step) % cols
-            sent.append(to_col(parts.at[part, col], parts.at[part, col], part_send.at[part, step], part_recv.at[part, col], peer))
+
+        @pl.loop(1, cols)
+        def _(step):
+            to_col(parts.at[part, col], parts.at[part, col], part_send.at[part, step], part_recv.at[part, col], (col + step) % cols)
 
     total = corr[col]
     for step in range(1, cols):
@@ -197,13 +206,16 @@
         both = product(pro_both, a_high[peer], ROW_BY_COL)
         return both[:BS] + both[BS:] + product(pro_high, a_low[peer], ROW_BY_COL)
 
-    @pl.loop(1, rows)
-    def _(step):
-        peer = row_after(row, far_first(step))
-        image_out[peer] = block(peer)
-        to_row(image_out.at[peer], image_in.at[row], image_send.at[step], image_recv.at[row], peer)
-
-    image = block(row)
+    @pl.loop(0, rows // GROUP_OUT)
+    def _(group):
+        steps = [group * GROUP_OUT + k + 1 for k in range(GROUP_OUT)]
+        peers = [row_after(row, far_first(step)) for step in steps]
+        for peer in peers:
+            image_out[peer] = block(peer)
+        for step, peer in zip(steps, peers):
+            @pl.when(peer != row)
+            def _():
+                to_row(image_out.at[peer], image_in.at[row], image_send.at[step], image_recv.at[row], peer)
 
     total = jnp.zeros_like(corr_rows[0])
     for source in range(rows):
@@ -216,6 +228,7 @@
         peer = (col + step) % cols
         sent.append(to_col(corr_whole.at[col], corr_whole.at[col], call_send.at[step], call_recv.at[col], peer))
 
+    image = image_out[row]
     for step in range(1, rows):
         source = row_before(row, step)
         arrive(image_in.at[source], image_recv.at[source])
@@ -288,6 +301,11 @@
 
     for copy in sent:
         copy.wait_send()
+
+    @pl.loop(1, cols)
+    def _(step):
+        for part in range(2):
+            arrive(parts.at[part, col], part_send.at[part, step])
 
     @pl.loop(1, rows)
     def _(step):

time: 48 us -> 47.3 us (0.985)
  Pallas kernels: 45.4 us -> 44.7 us
    pallas_call x1, Pallas kernels: 45.4 us -> 44.7 us  [local(): new_block, coefficients, factor = call(projection, basis)]
where the time goes in v4:
time: 47.3 us; the launch traced here: 47.2 us
  Pallas kernels  44.7 us (95%)
  local copies, waits for them, and re-layouts  1.81 us (4%)
  between operations  0.64 us (1%)
    pallas_call x1, Pallas kernels, local(): new_block, coefficients, factor = call(projection, basis)  44.7 us
    unnamed x3, local copies, waits for them, and re-layouts  1.81 us

profile of v4, /device:TPU:1, one launch (start us, length us, event | category | flops | bytes accessed | tf_op | source)
XLA Modules:
  0.0 47.2 jit_solution(6281286116472592080)
XLA Ops:
  0.6 44.7 %shard_map.49 = (f32[16,512]{1,0:T(8,128)S(1)}, f32[16,128]{1,0:T(8,128)S(1)}, f32[16,16]{1,0:T(8,128)S(1)}) custom-call(f32[512,8192]{1,0:T(8,128)} %a_hbm.1, f32[128,512]{1,0:T(8,128)} %basis_hbm.1), custom_call_target="tpu_custom_call" | custom-call | tf_op jit(solution)/shard_map/pallas_call | solution.py:358
  45.4 0.6 %copy.8 = f32[16,512]{1,0:T(8,128)} copy(f32[16,512]{1,0:T(8,128)S(1)} %get-tuple-element.12) | data formatting | bytes 65536
  46.0 0.6 %copy.9 = f32[128,16]{0,1:T(8,128)} copy(f32[128,16]{0,1:T(8,128)S(1)} %bitcast.1) | data formatting | bytes 16384
  46.6 0.6 %copy.10 = f32[16,16]{1,0:T(8,128)} copy(f32[16,16]{1,0:T(8,128)S(1)} %get-tuple-element.14) | data formatting | bytes 2048

commit v5 on v4

--- a/solution.py
+++ b/solution.py
@@ -217,6 +217,15 @@
             def _():
                 to_row(image_out.at[peer], image_in.at[row], image_send.at[step], image_recv.at[row], peer)
 
+    for copy in sent:
+        copy.wait_send()
+    sent = []
+
+    @pl.loop(1, cols)
+    def _(step):
+        for part in range(2):
+            arrive(parts.at[part, col], part_send.at[part, step])
+
     total = jnp.zeros_like(corr_rows[0])
     for source in range(rows):
         @pl.when(source != row)
@@ -229,7 +238,7 @@
         sent.append(to_col(corr_whole.at[col], corr_whole.at[col], call_send.at[step], call_recv.at[col], peer))
 
     image = image_out[row]
-    for step in range(1, rows):
+    for step in FAR_FIRST:
         source = row_before(row, step)
         arrive(image_in.at[source], image_recv.at[source])
         image += image_in[source]
@@ -261,20 +270,31 @@
     for source in range(1, cols):
         total += stat_cols[source]
     stat_rows[row] = total
+    last_sent = []
     for step in FAR_FIRST:
         peer = row_after(row, step)
-        sent.append(to_row(stat_rows.at[row], stat_rows.at[row], srow_send.at[step], srow_recv.at[row], peer))
+        last_sent.append(to_row(stat_rows.at[row], stat_rows.at[row], srow_send.at[step], srow_recv.at[row], peer))
+    for copy in sent:
+        copy.wait_send()
+    sent = []
+
+    @pl.loop(1, rows)
+    def _(step):
+        arrive(image_out.at[row_after(row, far_first(step))], image_send.at[step])
+
     for step in range(1, rows):
         source = row_before(row, step)
+        arrive(squares.at[source], square_recv.at[source])
+    square = squares[0]
+    for source in range(1, rows):
+        square += squares[source]
+
+    for step in FAR_FIRST:
+        source = row_before(row, step)
         arrive(stat_rows.at[source], srow_recv.at[source])
-        arrive(squares.at[source], square_recv.at[source])
     total = stat_rows[0]
     for source in range(1, rows):
         total += stat_rows[source]
-
-    square = squares[0]
-    for source in range(1, rows):
-        square += squares[source]
     cross = jnp.concatenate([total[:, : prior - BS], square[:, :BS]], 1)
     self_gram = total[:, prior - BS :]
     coeffs = exact(cross, double, ROW_BY_ROW)
@@ -288,7 +308,7 @@
     factor = jnp.zeros((BS, BS), f32)
     for j in range(BS):
         column = gram[:, j : j + 1]
-        scale = 1.0 / jnp.sqrt(column[j : j + 1])
+        scale = lax.rsqrt(column[j : j + 1])
         column = column * scale
         gram_line = gram[j : j + 1] * scale
         image_line = image[j : j + 1] * scale
@@ -299,17 +319,8 @@
     new_ref[...] = image
     factor_ref[...] = factor
 
-    for copy in sent:
+    for copy in last_sent:
         copy.wait_send()
-
-    @pl.loop(1, cols)
-    def _(step):
-        for part in range(2):
-            arrive(parts.at[part, col], part_send.at[part, step])
-
-    @pl.loop(1, rows)
-    def _(step):
-        arrive(image_out.at[row_after(row, step)], image_send.at[step])
 
 
 def local(rows, cols, projection, basis):

time: 47.3 us -> 46.8 us (0.989)
  Pallas kernels: 44.7 us -> 44.2 us
    pallas_call x1, Pallas kernels: 44.7 us -> 44.2 us  [local(): new_block, coefficients, factor = call(projection, basis)]
where the time goes in v5:
time: 46.8 us; the launch traced here: 46.7 us
  Pallas kernels  44.2 us (94%)
  local copies, waits for them, and re-layouts  1.81 us (4%)
  between operations  0.64 us (1%)
    pallas_call x1, Pallas kernels, local(): new_block, coefficients, factor = call(projection, basis)  44.2 us
    unnamed x3, local copies, waits for them, and re-layouts  1.81 us

profile of v5, /device:TPU:1, one launch (start us, length us, event | category | flops | bytes accessed | tf_op | source)
XLA Modules:
  0.0 46.7 jit_solution(15838653096964426832)
XLA Ops:
  0.6 44.2 %shard_map.49 = (f32[16,512]{1,0:T(8,128)S(1)}, f32[16,128]{1,0:T(8,128)S(1)}, f32[16,16]{1,0:T(8,128)S(1)}) custom-call(f32[512,8192]{1,0:T(8,128)} %a_hbm.1, f32[128,512]{1,0:T(8,128)} %basis_hbm.1), custom_call_target="tpu_custom_call" | custom-call | tf_op jit(solution)/shard_map/pallas_call | solution.py:369
  44.9 0.6 %copy.8 = f32[16,512]{1,0:T(8,128)} copy(f32[16,512]{1,0:T(8,128)S(1)} %get-tuple-element.12) | data formatting | bytes 65536
  45.5 0.6 %copy.9 = f32[128,16]{0,1:T(8,128)} copy(f32[128,16]{0,1:T(8,128)S(1)} %bitcast.1) | data formatting | bytes 16384
  46.1 0.6 %copy.10 = f32[16,16]{1,0:T(8,128)} copy(f32[16,16]{1,0:T(8,128)S(1)} %get-tuple-element.14) | data formatting | bytes 2048

commit v6 on v5

--- a/solution.py
+++ b/solution.py
@@ -16,7 +16,7 @@
 GROUP_OUT = 2
 SIDE = 4
 MESH = pl.DeviceIdType.MESH
-FAR_FIRST = [10, 6, 9, 14, 11, 5, 7, 13, 15, 8, 2, 1, 3, 4, 12]
+FAR_FIRST = [10, 6, 9, 14, 11, 5, 15, 7, 13, 8, 2, 1, 12, 3, 4]
 f32, bf16 = jnp.float32, jnp.bfloat16
 ROW_BY_ROW = (((1,), (1,)), ((), ()))
 ROW_BY_COL = (((1,), (0,)), ((), ()))
@@ -119,7 +119,7 @@
             fetch(block + depth).start()
 
     for block in range(depth):
-        fetch(block).start()
+        fetch(block).start(priority=1)
 
     @pl.loop(0, EARLY)
     def _(block):

time: 46.8 us -> 46.6 us (level)
  no operation moved by 1% of the time
where the time goes in v6:
time: 46.6 us; the launch traced here: 46.5 us
  Pallas kernels  44 us (94%)
  local copies, waits for them, and re-layouts  1.81 us (4%)
  between operations  0.64 us (1%)
    pallas_call x1, Pallas kernels, local(): new_block, coefficients, factor = call(projection, basis)  44 us
    unnamed x3, local copies, waits for them, and re-layouts  1.81 us

profile of v6, /device:TPU:1, one launch (start us, length us, event | category | flops | bytes accessed | tf_op | source)
XLA Modules:
  0.0 46.5 jit_solution(4137475350111755990)
XLA Ops:
  0.6 44.0 %shard_map.49 = (f32[16,512]{1,0:T(8,128)S(1)}, f32[16,128]{1,0:T(8,128)S(1)}, f32[16,16]{1,0:T(8,128)S(1)}) custom-call(f32[512,8192]{1,0:T(8,128)} %a_hbm.1, f32[128,512]{1,0:T(8,128)} %basis_hbm.1), custom_call_target="tpu_custom_call" | custom-call | tf_op jit(solution)/shard_map/pallas_call | solution.py:369
  44.7 0.6 %copy.8 = f32[16,512]{1,0:T(8,128)} copy(f32[16,512]{1,0:T(8,128)S(1)} %get-tuple-element.12) | data formatting | bytes 65536
  45.3 0.6 %copy.9 = f32[128,16]{0,1:T(8,128)} copy(f32[128,16]{0,1:T(8,128)S(1)} %bitcast.1) | data formatting | bytes 16384
  45.9 0.6 %copy.10 = f32[16,16]{1,0:T(8,128)} copy(f32[16,16]{1,0:T(8,128)S(1)} %get-tuple-element.14) | data formatting | bytes 2048

commit v7 on v5

--- a/solution.py
+++ b/solution.py
@@ -9,9 +9,9 @@
 
 N = 65536
 BS = 16
-DEPTH = 6
+DEPTH = 4
 EARLY = 3
-LAST = 6
+LAST = 9
 GROUP = 3
 GROUP_OUT = 2
 SIDE = 4

time: 46.8 us -> 46.5 us (level)
  no operation moved by 1% of the time
where the time goes in v7:
time: 46.5 us; the launch traced here: 46.3 us
  Pallas kernels  43.9 us (94%)
  local copies, waits for them, and re-layouts  1.81 us (4%)
  between operations  0.64 us (1%)
    pallas_call x1, Pallas kernels, local(): new_block, coefficients, factor = call(projection, basis)  43.9 us
    unnamed x3, local copies, waits for them, and re-layouts  1.81 us

profile of v7, /device:TPU:1, one launch (start us, length us, event | category | flops | bytes accessed | tf_op | source)
XLA Modules:
  0.0 46.3 jit_solution(4288410445975150312)
XLA Ops:
  0.6 43.9 %shard_map.49 = (f32[16,512]{1,0:T(8,128)S(1)}, f32[16,128]{1,0:T(8,128)S(1)}, f32[16,16]{1,0:T(8,128)S(1)}) custom-call(f32[512,8192]{1,0:T(8,128)} %a_hbm.1, f32[128,512]{1,0:T(8,128)} %basis_hbm.1), custom_call_target="tpu_custom_call" | custom-call | tf_op jit(solution)/shard_map/pallas_call | solution.py:369
  44.5 0.6 %copy.8 = f32[16,512]{1,0:T(8,128)} copy(f32[16,512]{1,0:T(8,128)S(1)} %get-tuple-element.12) | data formatting | bytes 65536
  45.1 0.6 %copy.9 = f32[128,16]{0,1:T(8,128)} copy(f32[128,16]{0,1:T(8,128)S(1)} %bitcast.1) | data formatting | bytes 16384
  45.7 0.6 %copy.10 = f32[16,16]{1,0:T(8,128)} copy(f32[16,16]{1,0:T(8,128)S(1)} %get-tuple-element.14) | data formatting | bytes 2048

commit v8 on v5

--- a/solution.py
+++ b/solution.py
@@ -16,7 +16,7 @@
 GROUP_OUT = 2
 SIDE = 4
 MESH = pl.DeviceIdType.MESH
-FAR_FIRST = [10, 6, 9, 14, 11, 5, 7, 13, 15, 8, 2, 1, 3, 4, 12]
+FAR_FIRST = [10, 6, 9, 14, 11, 8, 2, 5, 7, 13, 15, 1, 3, 4, 12]
 f32, bf16 = jnp.float32, jnp.bfloat16
 ROW_BY_ROW = (((1,), (1,)), ((), ()))
 ROW_BY_COL = (((1,), (0,)), ((), ()))

time: 46.8 us -> 46.7 us (level)
  no operation moved by 1% of the time
where the time goes in v8:
time: 46.7 us; the launch traced here: 46.6 us
  Pallas kernels  44.1 us (94%)
  local copies, waits for them, and re-layouts  1.81 us (4%)
  between operations  0.64 us (1%)
    pallas_call x1, Pallas kernels, local(): new_block, coefficients, factor = call(projection, basis)  44.1 us
    unnamed x3, local copies, waits for them, and re-layouts  1.81 us

profile of v8, /device:TPU:1, one launch (start us, length us, event | category | flops | bytes accessed | tf_op | source)
XLA Modules:
  0.0 46.6 jit_solution(14198962308853926942)
XLA Ops:
  0.6 44.1 %shard_map.49 = (f32[16,512]{1,0:T(8,128)S(1)}, f32[16,128]{1,0:T(8,128)S(1)}, f32[16,16]{1,0:T(8,128)S(1)}) custom-call(f32[512,8192]{1,0:T(8,128)} %a_hbm.1, f32[128,512]{1,0:T(8,128)} %basis_hbm.1), custom_call_target="tpu_custom_call" | custom-call | tf_op jit(solution)/shard_map/pallas_call | solution.py:369
  44.8 0.6 %copy.8 = f32[16,512]{1,0:T(8,128)} copy(f32[16,512]{1,0:T(8,128)S(1)} %get-tuple-element.12) | data formatting | bytes 65536
  45.4 0.6 %copy.9 = f32[128,16]{0,1:T(8,128)} copy(f32[128,16]{0,1:T(8,128)S(1)} %bitcast.1) | data formatting | bytes 16384
  46.0 0.6 %copy.10 = f32[16,16]{1,0:T(8,128)} copy(f32[16,16]{1,0:T(8,128)S(1)} %get-tuple-element.14) | data formatting | bytes 2048
